TPU v7x, 32 devices: a whole 2x2x4 slice. The times are simulated.
32 devices in a mesh: dp: 2 (over x), expert: 16 (over z, y, core).
Axes of the slice: x: 2, y: 2, z: 4, core: 2. Of those that a mesh axis runs over, the one named last changes fastest.
Arguments:
- tokens: bfloat16 [4096, 2048], P(('dp', 'expert')), may hold values from -6 to 6
- cotangent: bfloat16 [4096, 2048], P(('dp', 'expert')), may hold values from -6 to 6
- expert_ids: int32 [4096, 8], P(('dp', 'expert')), may hold values from 0 to 127, as said below
- gate_probs: float32 [4096, 8], P(('dp', 'expert')), may hold values from 0.1 to 1
- gate_weight: bfloat16 [16, 2048, 128], P('expert'), may hold values from -0.125 to 0.125
- up_weight: bfloat16 [16, 2048, 128], P('expert'), may hold values from -0.125 to 0.125
- down_weight: bfloat16 [16, 128, 2048], P('expert'), may hold values from -0.1875 to 0.1875
Outputs:
- grad_input: bfloat16 [4096, 2048], P(('dp', 'expert'))
- grad_gate: bfloat16 [16, 2048, 128], P('expert')
- grad_up: bfloat16 [16, 2048, 128], P('expert')
- grad_down: bfloat16 [16, 128, 2048], P('expert')
Inputs may be any that keep to these rules, and one draw needn't show every extreme that they name: `expert_ids`: each row names 8 different experts. Among the 128 rows of one device, each window expert 0 to 1 is named by 1 to 8 rows, and in every draw one window expert of every device is named by exactly 8 rows.
All inputs are finite; a program needn't handle non-finite values.
Results may differ from a plain program's by a relative error of at most 0.0064.
Values may be sent and summed in bfloat16 or wider, within the bound.
No kernel may reach another device: no remote copies, remote signals or barrier semaphores. Data moves between devices by JAX's collectives and lax.ppermute only.
A program may use at most 64 MiB of HBM per device.

v0:
```python
import jax
import jax.numpy as jnp
from jax import lax
from jax.sharding import PartitionSpec as P

SLICES = 8
CAP = 8


def silu_parts(gate_pre):
    sigmoid_value = jax.nn.sigmoid(gate_pre)
    return (gate_pre * sigmoid_value, sigmoid_value * (1.0 + gate_pre * (1.0 - sigmoid_value)))


def expert_slice(rows_in, rows_cot, gate_rows, up_rows, down_rows):
    gate_pre = jnp.dot(rows_in, gate_rows, preferred_element_type=jnp.float32)
    upward = jnp.dot(rows_in, up_rows, preferred_element_type=jnp.float32)
    swish, slope = silu_parts(gate_pre)
    active = (swish * upward).astype(jnp.bfloat16)
    dhidden = lax.dot_general(
        rows_cot, down_rows, (((1,), (1,)), ((), ())), preferred_element_type=jnp.float32
    )
    dgate = (dhidden * upward * slope).astype(jnp.bfloat16)
    dupward = (dhidden * swish).astype(jnp.bfloat16)
    grad_down = lax.dot_general(
        active, rows_cot, (((0,), (0,)), ((), ())), preferred_element_type=jnp.float32
    )
    grad_gate = lax.dot_general(
        rows_in, dgate, (((0,), (0,)), ((), ())), preferred_element_type=jnp.float32
    )
    grad_up = lax.dot_general(
        rows_in, dupward, (((0,), (0,)), ((), ())), preferred_element_type=jnp.float32
    )
    partial_value = lax.dot_general(
        dgate, gate_rows, (((1,), (1,)), ((), ())), preferred_element_type=jnp.float32
    )
    partial_value = partial_value + lax.dot_general(
        dupward, up_rows, (((1,), (1,)), ((), ())), preferred_element_type=jnp.float32
    )
    return (partial_value, grad_gate, grad_up, grad_down)


def local(tokens, cotangent, expert_ids, gate_probs, gate_weight, up_weight, down_weight):
    devices = lax.axis_size("expert")
    window = devices // SLICES
    capacity = CAP
    width = tokens.shape[1]
    local_rows = tokens.shape[0]
    matched = expert_ids[:, :, None] == jnp.arange(window, dtype=jnp.int32)[None, None, :]
    hit_count = jnp.sum(matched.astype(jnp.int32), axis=1)
    chosen = jnp.sum(jnp.where(matched, gate_probs[:, :, None], 0.0), axis=1)
    slot_rank = jnp.cumsum(hit_count, axis=0) - hit_count
    placed = (hit_count[:, :, None] == 1) & (
        slot_rank[:, :, None] == jnp.arange(capacity, dtype=jnp.int32)[None, None, :]
    )
    picker = placed.astype(jnp.bfloat16)
    filled = jnp.any(placed, axis=0)
    owner_row = jnp.sum(
        jnp.where(placed, jnp.arange(local_rows, dtype=jnp.int32)[:, None, None], 0), axis=0
    )
    slot_prob = jnp.sum(jnp.where(placed, chosen[:, :, None], 0.0), axis=0)
    rows_in = jnp.einsum("tec,td->ecd", picker, tokens, preferred_element_type=jnp.float32).astype(
        jnp.bfloat16
    )
    picked_cot = jnp.einsum("tec,td->ecd", picker, cotangent, preferred_element_type=jnp.float32)
    rows_cot = (slot_prob[:, :, None] * picked_cot).astype(jnp.bfloat16)
    gate_rows = gate_weight[0]
    up_rows = up_weight[0]
    down_rows = down_weight[0]
    send_in = jnp.broadcast_to(rows_in[None], (SLICES, window, capacity, width)).reshape(
        devices, capacity, width
    )
    send_cot = jnp.broadcast_to(rows_cot[None], (SLICES, window, capacity, width)).reshape(
        devices, capacity, width
    )
    recv_in, recv_cot = (
        lax.all_to_all(send_in, "expert", split_axis=0, concat_axis=0, tiled=True),
        lax.all_to_all(send_cot, "expert", split_axis=0, concat_axis=0, tiled=True),
    )
    partial_value, grad_g, grad_u, grad_d = expert_slice(
        recv_in.reshape(devices * capacity, width),
        recv_cot.reshape(devices * capacity, width),
        gate_rows,
        up_rows,
        down_rows,
    )
    returned = lax.all_to_all(
        partial_value.astype(jnp.bfloat16).reshape(devices, capacity, width),
        "expert",
        split_axis=0,
        concat_axis=0,
        tiled=True,
    )
    back = jnp.sum(returned.reshape(SLICES, window, capacity, width).astype(jnp.float32), axis=0)
    summed_g, summed_u, summed_d = lax.psum((grad_g, grad_u, grad_d), "dp")
    kept = jnp.where(filled[:, :, None], back, jnp.float32(0)).reshape(window * capacity, width)
    grad_rows = (
        jnp.zeros((local_rows, width), jnp.float32)
        .at[owner_row.reshape(window * capacity)]
        .add(kept)
    )
    grad_input = grad_rows.astype(jnp.bfloat16)
    return (
        grad_input,
        summed_g.astype(jnp.bfloat16)[None],
        summed_u.astype(jnp.bfloat16)[None],
        summed_d.astype(jnp.bfloat16)[None],
    )


def solution(mesh):
    placed = (
        P(("dp", "expert"), None),
        P(("dp", "expert"), None),
        P(("dp", "expert"), None),
        P(("dp", "expert"), None),
        P("expert", None, None),
        P("expert", None, None),
        P("expert", None, None),
    )
    return jax.shard_map(
        local,
        mesh=mesh,
        in_specs=placed,
        out_specs=(
            P(("dp", "expert"), None),
            P("expert", None, None),
            P("expert", None, None),
            P("expert", None, None),
        ),
        check_vma=False,
    )
```

profile of v0, /device:TPU:0, one launch (start us, length us, event | category | flops | bytes accessed | tf_op | source)
XLA Modules:
  0.0 133.9 jit_solution(7606036372887287696)
XLA Ops:
  0.6 0.8 convert_reduce_fusion.1
  1.5 0.2 reduce_window_sum.11
  1.8 1.2 convolution_convert_fusion
  3.0 0.9 broadcast_in_dim.95
  3.9 7.5 %all-to-all-start.1 = ((bf16[16,8,2048]{2,1,0:T(8,128)(2,1)}), bf16[16,8,2048]{2,1,0:T(8,128)(2,1)S(1)}, u32[]{:S(2)}, u32[]{:S(2)}) async-start(bf16[16,8,2048]{2,1,0:T(8,128)(2,1)} %bitcast.6), calls=%async_computation.1 | async-start | bytes 1048576 | tf_op jit(solution)/shard_map/all_to_all | solution.py:77
  11.6 0.2 fusion.2
  11.7 14.0 %all-to-all-done.1 = bf16[16,8,2048]{2,1,0:T(8,128)(2,1)S(1)} async-done(((bf16[16,8,2048]{2,1,0:T(8,128)(2,1)}), bf16[16,8,2048]{2,1,0:T(8,128)(2,1)S(1)}, u32[]{:S(2)}, u32[]{:S(2)}) %all-to-all-start.1) | async-done | bytes 524320 | tf_op jit(solution)/shard_map/all_to_all | solution.py:77
  25.7 0.8 broadcast_in_dim.94
  26.5 4.2 %all-to-all-start = ((bf16[16,8,2048]{2,1,0:T(8,128)(2,1)}), bf16[16,8,2048]{2,1,0:T(8,128)(2,1)S(1)}, u32[]{:S(2)}, u32[]{:S(2)}) async-start(bf16[16,8,2048]{2,1,0:T(8,128)(2,1)} %bitcast.2), calls=%async_computation | async-start | bytes 1048576 | tf_op jit(solution)/shard_map/all_to_all | solution.py:78
  31.2 0.3 fusion.5
  31.5 0.8 copy-done.1
  32.2 0.3 fusion.8
  32.6 12.4 %all-to-all-done = bf16[16,8,2048]{2,1,0:T(8,128)(2,1)S(1)} async-done(((bf16[16,8,2048]{2,1,0:T(8,128)(2,1)}), bf16[16,8,2048]{2,1,0:T(8,128)(2,1)S(1)}, u32[]{:S(2)}, u32[]{:S(2)}) %all-to-all-start) | async-done | bytes 524320 | tf_op jit(solution)/shard_map/all_to_all | solution.py:78
  45.0 1.3 %fusion.19 = f32[128,2048]{1,0:T(8,128)} fusion(bf16[16,8,2048]{2,1,0:T(8,128)(2,1)S(1)} %all-to-all-done, f32[128,128]{1,0:T(8,128)S(1)} %fusion.8, f32[128,128]{1,0:T(8,128)S(1)} %fusion.5), kind=kOutput, calls=%fused_computation.24 | convolution fusion | flops 67207168 | bytes 1703936 | tf_op jit(solution)/shard_map/dot_general | solution.py:25
  46.3 0.3 multiply_convert_fusion.1
  46.6 0.3 fusion.10
  47.0 0.3 fusion.3
  47.3 0.3 fusion.12
  47.6 0.7 copy-done.2
  48.3 1.1 fusion.1
  49.4 4.2 %all-to-all-start.2 = ((bf16[16,8,2048]{2,1,0:T(8,128)(2,1)}), bf16[16,8,2048]{2,1,0:T(8,128)(2,1)S(1)}, u32[]{:S(2)}, u32[]{:S(2)}) async-start(bf16[16,8,2048]{2,1,0:T(8,128)(2,1)} %fusion.1), calls=%async_computation.2 | async-start | bytes 1048576 | tf_op jit(solution)/shard_map/all_to_all | solution.py:87
  53.6 78.2 %all-reduce.2 = (bf16[2048,128]{1,0:T(8,128)(2,1)}, bf16[2048,128]{1,0:T(8,128)(2,1)}, bf16[128,2048]{1,0:T(8,128)(2,1)}) all-reduce(f32[2048,128]{1,0:T(8,128)S(1)} %fusion.12, f32[2048,128]{1,0:T(8,128)S(1)} %fusion.10, f32[128,2048]{1,0:T(8,128)} %fusion.19), channel_id=1, replica_groups=mesh['dp'=2,'expert'=16] {'dp'}, use_global_device_ids=true, to_apply=%region_8.9 | all-reduce | flops 786432 | bytes 4718592 | tf_op jit(solution)/shard_map/psum | solution.py:95
  131.9 1.1 scatter_custom_fusion
  133.0 0.9 convert_element_type.48
  (25 shorter events, 0.9 us)
Async XLA Ops:
  0.6 30.6 %copy-start = (bf16[1,2048,128]{2,1,0:T(8,128)(2,1)S(1)}, bf16[1,2048,128]{2,1,0:T(8,128)(2,1)}, u32[]{:S(2)}) copy-start(bf16[1,2048,128]{2,1,0:T(8,128)(2,1)} %param.11) | copy-start | bytes 1572868
  3.9 7.6 %copy-start.4 = (s32[128,8]{0,1:T(8,128)S(1)}, s32[128,8]{0,1:T(8,128)}, u32[]{:S(2)}) copy-start(s32[128,8]{0,1:T(8,128)} %param.9) | copy-start | bytes 12292
  3.9 7.6 %copy-start.5 = (f32[128,8]{0,1:T(8,128)S(1)}, f32[128,8]{0,1:T(8,128)}, u32[]{:S(2)}) copy-start(f32[128,8]{0,1:T(8,128)} %param.10) | copy-start | bytes 12292
  3.9 7.7 %copy-start.3 = (bf16[128,2048]{1,0:T(8,128)(2,1)S(1)}, bf16[128,2048]{1,0:T(8,128)(2,1)}, u32[]{:S(2)}) copy-start(bf16[128,2048]{1,0:T(8,128)(2,1)} %param.8) | copy-start | bytes 1572868
  3.9 21.8 %all-to-all-start.1 = ((bf16[16,8,2048]{2,1,0:T(8,128)(2,1)}), bf16[16,8,2048]{2,1,0:T(8,128)(2,1)S(1)}, u32[]{:S(2)}, u32[]{:S(2)}) async-start(bf16[16,8,2048]{2,1,0:T(8,128)(2,1)} %bitcast.6), calls=%async_computation.1 | async-start | bytes 1048576 | tf_op jit(solution)/shard_map/all_to_all | solution.py:77
  26.5 18.4 %all-to-all-start = ((bf16[16,8,2048]{2,1,0:T(8,128)(2,1)}), bf16[16,8,2048]{2,1,0:T(8,128)(2,1)S(1)}, u32[]{:S(2)}, u32[]{:S(2)}) async-start(bf16[16,8,2048]{2,1,0:T(8,128)(2,1)} %bitcast.2), calls=%async_computation | async-start | bytes 1048576 | tf_op jit(solution)/shard_map/all_to_all | solution.py:78
  31.2 1.1 copy-start.1
  32.5 13.8 %copy-start.6 = (bf16[1,128,2048]{2,1,0:T(8,128)(2,1)S(1)}, bf16[1,128,2048]{2,1,0:T(8,128)(2,1)}, u32[]{:S(2)}) copy-start(bf16[1,128,2048]{2,1,0:T(8,128)(2,1)} %param.13) | copy-start | bytes 1572868
  47.3 1.0 copy-start.2
  49.4 82.4 %all-to-all-start.2 = ((bf16[16,8,2048]{2,1,0:T(8,128)(2,1)}), bf16[16,8,2048]{2,1,0:T(8,128)(2,1)S(1)}, u32[]{:S(2)}, u32[]{:S(2)}) async-start(bf16[16,8,2048]{2,1,0:T(8,128)(2,1)} %fusion.1), calls=%async_computation.2 | async-start | bytes 1048576 | tf_op jit(solution)/shard_map/all_to_all | solution.py:87
where the time goes:
time: 135 us; the launch traced here: 134 us
  blocking collectives  78.2 us (58%)
  waiting for transfers between devices  26.4 us (20%)
  starting transfers between devices  15.9 us (12%)
  matrix products  5.7 us (4%)
  local copies, waits for them, and re-layouts  3.51 us (3%)
  other arithmetic  3.4 us (3%)
    psum x1, blocking collectives, local(): summed_g, summed_u, summed_d = lax.psum((grad_g, grad_u, grad_d), 'dp')  78.2 us
    all_to_all x1, waiting for transfers between devices, local(): lax.all_to_all(send_in, 'expert', split_axis=0, concat_axis=0, tiled=True)  14 us
    all_to_all x1, waiting for transfers between devices, local(): lax.all_to_all(send_cot, 'expert', split_axis=0, concat_axis=0, tiled=True)  12.4 us
    all_to_all x1, starting transfers between devices, local(): lax.all_to_all(send_in, 'expert', split_axis=0, concat_axis=0, tiled=True)  7.55 us
    all_to_all x1, starting transfers between devices, local(): lax.all_to_all(send_cot, 'expert', split_axis=0, concat_axis=0, tiled=True)  4.16 us
    all_to_all x1, starting transfers between devices, local(): lax.all_to_all(partial_value.astype(jnp.bfloat16).reshape(devices, capaci...  4.16 us
  transfers between devices with their start and end apart: 3, of which 2 were waited for; matrix products, arithmetic and copies ran while one was open for 1% of the time, Pallas kernels for 0%

commit v1 on v0

--- a/solution.py
+++ b/solution.py
@@ -73,9 +73,33 @@
     send_cot = jnp.broadcast_to(rows_cot[None], (SLICES, window, capacity, width)).reshape(
         devices, capacity, width
     )
+
+    def wrap_units(vec, axis_key):
+        v_next = lax.psum(1, axis_name=axis_key)
+        side_arr, prior = (v_next, lax.axis_index(axis_key))
+        f_next = vec.shape[0] // side_arr
+        met_up = list(vec.shape)
+        met_up[0] = f_next
+        block_last = met_up[0]
+        met_up[0] = block_last * side_arr
+        built = jnp.zeros(met_up, vec.dtype)
+        for src_i in range(side_arr):
+            arr_now = lax.dynamic_slice_in_dim(vec, (prior ^ src_i) * f_next, f_next, axis=0)
+            if src_i:
+                known = range(side_arr)
+                arr_now = lax.ppermute(
+                    arr_now,
+                    axis_name=axis_key,
+                    perm=list(map(lambda nth: (nth, nth ^ src_i), known)),
+                )
+            built = lax.dynamic_update_slice_in_dim(
+                built, arr_now, (prior ^ src_i) * block_last, axis=0
+            )
+        return built
+
     recv_in, recv_cot = (
         lax.all_to_all(send_in, "expert", split_axis=0, concat_axis=0, tiled=True),
-        lax.all_to_all(send_cot, "expert", split_axis=0, concat_axis=0, tiled=True),
+        wrap_units(send_cot, "expert"),
     )
     partial_value, grad_g, grad_u, grad_d = expert_slice(
         recv_in.reshape(devices * capacity, width),

time: 135 us -> 158 us (1.17)
  waiting for transfers between devices: 26.4 us -> 42.4 us
  starting transfers between devices: 15.9 us -> 23.4 us
    ppermute x0 -> x15, waiting for transfers between devices: none -> 42.4 us  [wrap_units(): lax.ppermute(arr_now, axis_name=axis_key, perm=list(map(lambda nth: (nth,...]
    all_to_all x1, waiting for transfers between devices: 14 us -> 0.01 us  [local(): lax.all_to_all(send_in, 'expert', split_axis=0, concat_axis=0, tiled=True)]
    all_to_all x1 -> x0, waiting for transfers between devices: 12.4 us -> none  [local(): lax.all_to_all(send_cot, 'expert', split_axis=0, concat_axis=0, tiled=True)]
    ppermute x0 -> x15, starting transfers between devices: none -> 12.1 us  [wrap_units(): lax.ppermute(arr_now, axis_name=axis_key, perm=list(map(lambda nth: (nth,...]
    all_to_all x1 -> x0, starting transfers between devices: 4.16 us -> none  [local(): lax.all_to_all(send_cot, 'expert', split_axis=0, concat_axis=0, tiled=True)]
  transfers between devices with their start and end apart: 3 -> 17, of which waited for: 2 -> 11; matrix products, arithmetic and copies ran while one was open for 1% -> 1% of each run, Pallas kernels for 0% -> 0%
where the time goes in v1:
time: 158 us
  blocking collectives  78.2 us (49%)
  waiting for transfers between devices  42.4 us (27%)
  starting transfers between devices  23.4 us (15%)
  matrix products  5.67 us (4%)
  local copies, waits for them, and re-layouts  3.61 us (2%)
  other arithmetic  3.4 us (2%)
    psum x1, blocking collectives, local(): summed_g, summed_u, summed_d = lax.psum((grad_g, grad_u, grad_d), 'dp')  78.2 us
    ppermute x15, waiting for transfers between devices, wrap_units(): lax.ppermute(arr_now, axis_name=axis_key, perm=list(map(lambda nth: (nth,...  42.4 us
    ppermute x15, starting transfers between devices, wrap_units(): lax.ppermute(arr_now, axis_name=axis_key, perm=list(map(lambda nth: (nth,...  12.1 us
    all_to_all x1, starting transfers between devices, local(): lax.all_to_all(send_in, 'expert', split_axis=0, concat_axis=0, tiled=True)  7.55 us
    all_to_all x1, starting transfers between devices, local(): lax.all_to_all(partial_value.astype(jnp.bfloat16).reshape(devices, capaci...  3.82 us
  transfers between devices with their start and end apart: 17, of which 11 were waited for; matrix products, arithmetic and copies ran while one was open for 1% of the time, Pallas kernels for 0%

profile of v1, /device:TPU:0, one launch (start us, length us, event | category | flops | bytes accessed | tf_op | source)
XLA Modules:
  0.0 157.7 jit_solution(628766871353325943)
XLA Ops:
  0.6 0.8 convert_reduce_fusion.1
  1.8 1.2 convolution_convert_fusion
  3.0 0.9 broadcast_in_dim.99
  3.9 7.5 %all-to-all-start = ((bf16[16,8,2048]{2,1,0:T(8,128)(2,1)}), bf16[16,8,2048]{2,1,0:T(8,128)(2,1)S(1)}, u32[]{:S(2)}, u32[]{:S(2)}) async-start(bf16[16,8,2048]{2,1,0:T(8,128)(2,1)} %bitcast.6), calls=%async_computation | async-start | bytes 1048576 | tf_op jit(solution)/shard_map/all_to_all | solution.py:101
  12.7 4.3 %collective-permute-start.14 = (bf16[1,8,2048]{2,1,0:T(8,128)(2,1)S(1)}, bf16[1,8,2048]{2,1,0:T(8,128)(2,1)S(1)}, u32[]{:S(2)}, u32[]{:S(2)}) collective-permute-start(bf16[1,8,2048]{2,1,0:T(8,128)(2,1)S(1)} %get-tuple-element.7), channel_id=1, source_target_pairs={{0,15},{1,14},{2,13},{3,12},{4,11},{5,10},{6,9},{7,8},{8,7},{9,6},... | collective-permute-start | bytes 98312 | tf_op jit(solution)/shard_map/ppermute | solution.py:90
  17.5 3.2 %collective-permute-start.12 = (bf16[1,8,2048]{2,1,0:T(8,128)(2,1)S(1)}, bf16[1,8,2048]{2,1,0:T(8,128)(2,1)S(1)}, u32[]{:S(2)}, u32[]{:S(2)}) collective-permute-start(bf16[1,8,2048]{2,1,0:T(8,128)(2,1)S(1)} %get-tuple-element.9), channel_id=1, source_target_pairs={{0,13},{1,12},{2,15},{3,14},{4,9},{5,8},{6,11},{7,10},{8,5},{9,4},... | collective-permute-start | bytes 98312 | tf_op jit(solution)/shard_map/ppermute | solution.py:90
  22.1 1.7 %collective-permute-start.1 = (bf16[1,8,2048]{2,1,0:T(8,128)(2,1)S(1)}, bf16[1,8,2048]{2,1,0:T(8,128)(2,1)S(1)}, u32[]{:S(2)}, u32[]{:S(2)}) collective-permute-start(bf16[1,8,2048]{2,1,0:T(8,128)(2,1)S(1)} %get-tuple-element.20), channel_id=1, source_target_pairs={{0,2},{1,3},{2,0},{3,1},{4,6},{5,7},{6,4},{7,5},{8,10},{9,11},{10,... | collective-permute-start | bytes 98312 | tf_op jit(solution)/shard_map/ppermute | solution.py:90
  23.9 3.7 %collective-permute-done.1 = bf16[1,8,2048]{2,1,0:T(8,128)(2,1)S(1)} collective-permute-done((bf16[1,8,2048]{2,1,0:T(8,128)(2,1)S(1)}, bf16[1,8,2048]{2,1,0:T(8,128)(2,1)S(1)}, u32[]{:S(2)}, u32[]{:S(2)}) %collective-permute-start.1) | collective-permute-done | bytes 32800 | tf_op jit(solution)/shard_map/ppermute | solution.py:90
  27.6 3.7 %collective-permute-done.2 = bf16[1,8,2048]{2,1,0:T(8,128)(2,1)S(1)} collective-permute-done((bf16[1,8,2048]{2,1,0:T(8,128)(2,1)S(1)}, bf16[1,8,2048]{2,1,0:T(8,128)(2,1)S(1)}, u32[]{:S(2)}, u32[]{:S(2)}) %collective-permute-start.2) | collective-permute-done | bytes 32800 | tf_op jit(solution)/shard_map/ppermute | solution.py:90
  31.3 3.9 %collective-permute-done.3 = bf16[1,8,2048]{2,1,0:T(8,128)(2,1)S(1)} collective-permute-done((bf16[1,8,2048]{2,1,0:T(8,128)(2,1)S(1)}, bf16[1,8,2048]{2,1,0:T(8,128)(2,1)S(1)}, u32[]{:S(2)}, u32[]{:S(2)}) %collective-permute-start.3) | collective-permute-done | bytes 32800 | tf_op jit(solution)/shard_map/ppermute | solution.py:90
  35.2 3.3 %collective-permute-done.4 = bf16[1,8,2048]{2,1,0:T(8,128)(2,1)S(1)} collective-permute-done((bf16[1,8,2048]{2,1,0:T(8,128)(2,1)S(1)}, bf16[1,8,2048]{2,1,0:T(8,128)(2,1)S(1)}, u32[]{:S(2)}, u32[]{:S(2)}) %collective-permute-start.4) | collective-permute-done | bytes 32800 | tf_op jit(solution)/shard_map/ppermute | solution.py:90
  38.6 4.8 %collective-permute-done.5 = bf16[1,8,2048]{2,1,0:T(8,128)(2,1)S(1)} collective-permute-done((bf16[1,8,2048]{2,1,0:T(8,128)(2,1)S(1)}, bf16[1,8,2048]{2,1,0:T(8,128)(2,1)S(1)}, u32[]{:S(2)}, u32[]{:S(2)}) %collective-permute-start.5) | collective-permute-done | bytes 32800 | tf_op jit(solution)/shard_map/ppermute | solution.py:90
  43.4 4.2 %collective-permute-done.6 = bf16[1,8,2048]{2,1,0:T(8,128)(2,1)S(1)} collective-permute-done((bf16[1,8,2048]{2,1,0:T(8,128)(2,1)S(1)}, bf16[1,8,2048]{2,1,0:T(8,128)(2,1)S(1)}, u32[]{:S(2)}, u32[]{:S(2)}) %collective-permute-start.6) | collective-permute-done | bytes 32800 | tf_op jit(solution)/shard_map/ppermute | solution.py:90
  48.3 4.1 %collective-permute-done.7 = bf16[1,8,2048]{2,1,0:T(8,128)(2,1)S(1)} collective-permute-done((bf16[1,8,2048]{2,1,0:T(8,128)(2,1)S(1)}, bf16[1,8,2048]{2,1,0:T(8,128)(2,1)S(1)}, u32[]{:S(2)}, u32[]{:S(2)}) %collective-permute-start.7) | collective-permute-done | bytes 32800 | tf_op jit(solution)/shard_map/ppermute | solution.py:90
  52.4 4.4 %collective-permute-done.8 = bf16[1,8,2048]{2,1,0:T(8,128)(2,1)S(1)} collective-permute-done((bf16[1,8,2048]{2,1,0:T(8,128)(2,1)S(1)}, bf16[1,8,2048]{2,1,0:T(8,128)(2,1)S(1)}, u32[]{:S(2)}, u32[]{:S(2)}) %collective-permute-start.8) | collective-permute-done | bytes 32800 | tf_op jit(solution)/shard_map/ppermute | solution.py:90
  56.8 1.2 collective-permute-start.9
  58.0 4.5 %collective-permute-done.9 = bf16[1,8,2048]{2,1,0:T(8,128)(2,1)S(1)} collective-permute-done((bf16[1,8,2048]{2,1,0:T(8,128)(2,1)S(1)}, bf16[1,8,2048]{2,1,0:T(8,128)(2,1)S(1)}, u32[]{:S(2)}, u32[]{:S(2)}) %collective-permute-start.9) | collective-permute-done | bytes 32800 | tf_op jit(solution)/shard_map/ppermute | solution.py:90
  62.6 5.1 %collective-permute-done.10 = bf16[1,8,2048]{2,1,0:T(8,128)(2,1)S(1)} collective-permute-done((bf16[1,8,2048]{2,1,0:T(8,128)(2,1)S(1)}, bf16[1,8,2048]{2,1,0:T(8,128)(2,1)S(1)}, u32[]{:S(2)}, u32[]{:S(2)}) %collective-permute-start.10) | collective-permute-done | bytes 32800 | tf_op jit(solution)/shard_map/ppermute | solution.py:90
  69.2 1.3 fusion.19
  72.5 1.1 fusion.1
  73.6 3.8 %all-to-all-start.1 = ((bf16[16,8,2048]{2,1,0:T(8,128)(2,1)}), bf16[16,8,2048]{2,1,0:T(8,128)(2,1)S(1)}, u32[]{:S(2)}, u32[]{:S(2)}) async-start(bf16[16,8,2048]{2,1,0:T(8,128)(2,1)} %fusion.1), calls=%async_computation.1 | async-start | bytes 1048576 | tf_op jit(solution)/shard_map/all_to_all | solution.py:111
  77.4 78.2 %all-reduce.2 = (bf16[2048,128]{1,0:T(8,128)(2,1)}, bf16[2048,128]{1,0:T(8,128)(2,1)}, bf16[128,2048]{1,0:T(8,128)(2,1)}) all-reduce(f32[2048,128]{1,0:T(8,128)S(1)} %fusion.12, f32[2048,128]{1,0:T(8,128)S(1)} %fusion.10, f32[128,2048]{1,0:T(8,128)} %fusion.19), channel_id=1, replica_groups=mesh['dp'=2,'expert'=16] {'dp'}, use_global_device_ids=true, to_apply=%region_8.9 | all-reduce | flops 786432 | bytes 4718592 | tf_op jit(solution)/shard_map/psum | solution.py:119
  155.7 1.1 scatter_custom_fusion
  156.8 0.9 convert_element_type.48
  (70 shorter events, 7.6 us)
Async XLA Ops:
  0.6 67.2 %copy-start = (bf16[1,2048,128]{2,1,0:T(8,128)(2,1)S(1)}, bf16[1,2048,128]{2,1,0:T(8,128)(2,1)}, u32[]{:S(2)}) copy-start(bf16[1,2048,128]{2,1,0:T(8,128)(2,1)} %param.11) | copy-start | bytes 1572868
  3.9 8.4 %copy-start.3 = (bf16[128,2048]{1,0:T(8,128)(2,1)S(1)}, bf16[128,2048]{1,0:T(8,128)(2,1)}, u32[]{:S(2)}) copy-start(bf16[128,2048]{1,0:T(8,128)(2,1)} %param.8) | copy-start | bytes 1572868
  3.9 64.0 %all-to-all-start = ((bf16[16,8,2048]{2,1,0:T(8,128)(2,1)}), bf16[16,8,2048]{2,1,0:T(8,128)(2,1)S(1)}, u32[]{:S(2)}, u32[]{:S(2)}) async-start(bf16[16,8,2048]{2,1,0:T(8,128)(2,1)} %bitcast.6), calls=%async_computation | async-start | bytes 1048576 | tf_op jit(solution)/shard_map/all_to_all | solution.py:101
  11.5 0.7 copy-start.5
  11.5 0.7 copy-start.4
  12.7 55.0 %collective-permute-start.14 = (bf16[1,8,2048]{2,1,0:T(8,128)(2,1)S(1)}, bf16[1,8,2048]{2,1,0:T(8,128)(2,1)S(1)}, u32[]{:S(2)}, u32[]{:S(2)}) collective-permute-start(bf16[1,8,2048]{2,1,0:T(8,128)(2,1)S(1)} %get-tuple-element.7), channel_id=1, source_target_pairs={{0,15},{1,14},{2,13},{3,12},{4,11},{5,10},{6,9},{7,8},{8,7},{9,6},... | collective-permute-start | bytes 98312 | tf_op jit(solution)/shard_map/ppermute | solution.py:90
  17.1 50.7 %collective-permute-start.13 = (bf16[1,8,2048]{2,1,0:T(8,128)(2,1)S(1)}, bf16[1,8,2048]{2,1,0:T(8,128)(2,1)S(1)}, u32[]{:S(2)}, u32[]{:S(2)}) collective-permute-start(bf16[1,8,2048]{2,1,0:T(8,128)(2,1)S(1)} %get-tuple-element.8), channel_id=1, source_target_pairs={{0,14},{1,15},{2,12},{3,13},{4,10},{5,11},{6,8},{7,9},{8,6},{9,7},... | collective-permute-start | bytes 98312 | tf_op jit(solution)/shard_map/ppermute | solution.py:90
  17.5 50.3 %collective-permute-start.12 = (bf16[1,8,2048]{2,1,0:T(8,128)(2,1)S(1)}, bf16[1,8,2048]{2,1,0:T(8,128)(2,1)S(1)}, u32[]{:S(2)}, u32[]{:S(2)}) collective-permute-start(bf16[1,8,2048]{2,1,0:T(8,128)(2,1)S(1)} %get-tuple-element.9), channel_id=1, source_target_pairs={{0,13},{1,12},{2,15},{3,14},{4,9},{5,8},{6,11},{7,10},{8,5},{9,4},... | collective-permute-start | bytes 98312 | tf_op jit(solution)/shard_map/ppermute | solution.py:90
  20.6 47.1 %collective-permute-start.11 = (bf16[1,8,2048]{2,1,0:T(8,128)(2,1)S(1)}, bf16[1,8,2048]{2,1,0:T(8,128)(2,1)S(1)}, u32[]{:S(2)}, u32[]{:S(2)}) collective-permute-start(bf16[1,8,2048]{2,1,0:T(8,128)(2,1)S(1)} %get-tuple-element.10), channel_id=1, source_target_pairs={{0,12},{1,13},{2,14},{3,15},{4,8},{5,9},{6,10},{7,11},{8,4},{9,5},... | collective-permute-start | bytes 98312 | tf_op jit(solution)/shard_map/ppermute | solution.py:90
  20.9 1.2 collective-permute-start
  22.1 5.5 %collective-permute-start.1 = (bf16[1,8,2048]{2,1,0:T(8,128)(2,1)S(1)}, bf16[1,8,2048]{2,1,0:T(8,128)(2,1)S(1)}, u32[]{:S(2)}, u32[]{:S(2)}) collective-permute-start(bf16[1,8,2048]{2,1,0:T(8,128)(2,1)S(1)} %get-tuple-element.20), channel_id=1, source_target_pairs={{0,2},{1,3},{2,0},{3,1},{4,6},{5,7},{6,4},{7,5},{8,10},{9,11},{10,... | collective-permute-start | bytes 98312 | tf_op jit(solution)/shard_map/ppermute | solution.py:90
  27.6 3.7 %collective-permute-start.2 = (bf16[1,8,2048]{2,1,0:T(8,128)(2,1)S(1)}, bf16[1,8,2048]{2,1,0:T(8,128)(2,1)S(1)}, u32[]{:S(2)}, u32[]{:S(2)}) collective-permute-start(bf16[1,8,2048]{2,1,0:T(8,128)(2,1)S(1)} %get-tuple-element.19), channel_id=1, source_target_pairs={{0,3},{1,2},{2,1},{3,0},{4,7},{5,6},{6,5},{7,4},{8,11},{9,10},{10,... | collective-permute-start | bytes 98312 | tf_op jit(solution)/shard_map/ppermute | solution.py:90
  31.3 3.9 %collective-permute-start.3 = (bf16[1,8,2048]{2,1,0:T(8,128)(2,1)S(1)}, bf16[1,8,2048]{2,1,0:T(8,128)(2,1)S(1)}, u32[]{:S(2)}, u32[]{:S(2)}) collective-permute-start(bf16[1,8,2048]{2,1,0:T(8,128)(2,1)S(1)} %get-tuple-element.18), channel_id=1, source_target_pairs={{0,4},{1,5},{2,6},{3,7},{4,0},{5,1},{6,2},{7,3},{8,12},{9,13},{10,... | collective-permute-start | bytes 98312 | tf_op jit(solution)/shard_map/ppermute | solution.py:90
  35.2 3.3 %collective-permute-start.4 = (bf16[1,8,2048]{2,1,0:T(8,128)(2,1)S(1)}, bf16[1,8,2048]{2,1,0:T(8,128)(2,1)S(1)}, u32[]{:S(2)}, u32[]{:S(2)}) collective-permute-start(bf16[1,8,2048]{2,1,0:T(8,128)(2,1)S(1)} %get-tuple-element.17), channel_id=1, source_target_pairs={{0,5},{1,4},{2,7},{3,6},{4,1},{5,0},{6,3},{7,2},{8,13},{9,12},{10,... | collective-permute-start | bytes 98312 | tf_op jit(solution)/shard_map/ppermute | solution.py:90
  38.5 4.8 %collective-permute-start.5 = (bf16[1,8,2048]{2,1,0:T(8,128)(2,1)S(1)}, bf16[1,8,2048]{2,1,0:T(8,128)(2,1)S(1)}, u32[]{:S(2)}, u32[]{:S(2)}) collective-permute-start(bf16[1,8,2048]{2,1,0:T(8,128)(2,1)S(1)} %get-tuple-element.16), channel_id=1, source_target_pairs={{0,6},{1,7},{2,4},{3,5},{4,2},{5,3},{6,0},{7,1},{8,14},{9,15},{10,... | collective-permute-start | bytes 98312 | tf_op jit(solution)/shard_map/ppermute | solution.py:90
  43.3 4.2 %collective-permute-start.6 = (bf16[1,8,2048]{2,1,0:T(8,128)(2,1)S(1)}, bf16[1,8,2048]{2,1,0:T(8,128)(2,1)S(1)}, u32[]{:S(2)}, u32[]{:S(2)}) collective-permute-start(bf16[1,8,2048]{2,1,0:T(8,128)(2,1)S(1)} %get-tuple-element.15), channel_id=1, source_target_pairs={{0,7},{1,6},{2,5},{3,4},{4,3},{5,2},{6,1},{7,0},{8,15},{9,14},{10,... | collective-permute-start | bytes 98312 | tf_op jit(solution)/shard_map/ppermute | solution.py:90
  47.6 4.8 %collective-permute-start.7 = (bf16[1,8,2048]{2,1,0:T(8,128)(2,1)S(1)}, bf16[1,8,2048]{2,1,0:T(8,128)(2,1)S(1)}, u32[]{:S(2)}, u32[]{:S(2)}) collective-permute-start(bf16[1,8,2048]{2,1,0:T(8,128)(2,1)S(1)} %get-tuple-element.14), channel_id=1, source_target_pairs={{0,8},{1,9},{2,10},{3,11},{4,12},{5,13},{6,14},{7,15},{8,0},{9,1},... | collective-permute-start | bytes 98312 | tf_op jit(solution)/shard_map/ppermute | solution.py:90
  52.4 4.4 %collective-permute-start.8 = (bf16[1,8,2048]{2,1,0:T(8,128)(2,1)S(1)}, bf16[1,8,2048]{2,1,0:T(8,128)(2,1)S(1)}, u32[]{:S(2)}, u32[]{:S(2)}) collective-permute-start(bf16[1,8,2048]{2,1,0:T(8,128)(2,1)S(1)} %get-tuple-element.13), channel_id=1, source_target_pairs={{0,9},{1,8},{2,11},{3,10},{4,13},{5,12},{6,15},{7,14},{8,1},{9,0},... | collective-permute-start | bytes 98312 | tf_op jit(solution)/shard_map/ppermute | solution.py:90
  56.8 5.7 %collective-permute-start.9 = (bf16[1,8,2048]{2,1,0:T(8,128)(2,1)S(1)}, bf16[1,8,2048]{2,1,0:T(8,128)(2,1)S(1)}, u32[]{:S(2)}, u32[]{:S(2)}) collective-permute-start(bf16[1,8,2048]{2,1,0:T(8,128)(2,1)S(1)} %get-tuple-element.12), channel_id=1, source_target_pairs={{0,10},{1,11},{2,8},{3,9},{4,14},{5,15},{6,12},{7,13},{8,2},{9,3},... | collective-permute-start | bytes 98312 | tf_op jit(solution)/shard_map/ppermute | solution.py:90
  62.6 5.1 %collective-permute-start.10 = (bf16[1,8,2048]{2,1,0:T(8,128)(2,1)S(1)}, bf16[1,8,2048]{2,1,0:T(8,128)(2,1)S(1)}, u32[]{:S(2)}, u32[]{:S(2)}) collective-permute-start(bf16[1,8,2048]{2,1,0:T(8,128)(2,1)S(1)} %get-tuple-element.11), channel_id=1, source_target_pairs={{0,11},{1,10},{2,9},{3,8},{4,15},{5,14},{6,13},{7,12},{8,3},{9,2},... | collective-permute-start | bytes 98312 | tf_op jit(solution)/shard_map/ppermute | solution.py:90
  67.8 1.0 copy-start.1
  69.1 1.3 copy-start.6
  71.4 1.0 copy-start.2
  73.6 82.1 %all-to-all-start.1 = ((bf16[16,8,2048]{2,1,0:T(8,128)(2,1)}), bf16[16,8,2048]{2,1,0:T(8,128)(2,1)S(1)}, u32[]{:S(2)}, u32[]{:S(2)}) async-start(bf16[16,8,2048]{2,1,0:T(8,128)(2,1)} %fusion.1), calls=%async_computation.1 | async-start | bytes 1048576 | tf_op jit(solution)/shard_map/all_to_all | solution.py:111
